TPU v7x, 32 devices: a whole 2x2x4 slice. The times are simulated.
32 devices in a mesh: bas: 8 (over y, x, core), aux: 4 (over z).
Axes of the slice: x: 2, y: 2, z: 4, core: 2. Of those that a mesh axis runs over, the one named last changes fastest.
Arguments:
- integrals: bfloat16 [4, 8192, 8192], P('aux', 'bas'), may hold values from -6 to 6
- screen: int32 [4, 64, 64], P('aux', 'bas'), may hold values from 0 to 1, as said below
- coefficients: bfloat16 [8192, 384], P('bas'), may hold values from -0.0625 to 0.0625
- weights: float32 [384], replicated, may hold values from -2 to 2
Outputs:
- exchange: bfloat16 [8192, 8192], P('aux', 'bas')
Inputs may be any that keep to these rules, and one draw needn't show every extreme that they name: `screen`: every block with equal row and column block index is 1; the share of ones differs from row block to row block.
All inputs are finite; a program needn't handle non-finite values.
Results may differ from a plain program's by a relative error of at most 0.018.
Values may be sent and summed in bfloat16 or wider, within the bound.
A program may use at most 128 MiB of HBM per device.

v0:
```python
import math
import jax
import jax.numpy as jnp
from jax import lax
from jax.sharding import PartitionSpec as P

NOCC = 384
BLOCK = 128
AUX_DEV = 1


def spread_2(block, axis, owner):
    block = jnp.where(lax.axis_index(axis) == owner, block, jnp.zeros_like(block))
    return lax.psum(block, axis)


def shards(integrals, screen, coefficients, weights):
    aux_count = integrals.shape[0]
    row_count = integrals.shape[1]
    basis_count = integrals.shape[2]
    occ_count = coefficients.shape[1]
    row_blocks = row_count // BLOCK
    col_blocks = basis_count // BLOCK
    masks = screen.reshape(aux_count, row_blocks, 1, col_blocks, 1).astype(jnp.bfloat16)
    masked = integrals.reshape(aux_count, row_blocks, BLOCK, col_blocks, BLOCK) * masks
    flat = masked.reshape(aux_count * row_count, basis_count)
    summed_half = jnp.dot(
        flat,
        lax.all_gather(coefficients, "bas", axis=0, tiled=True),
        preferred_element_type=jnp.float32,
    )
    half = summed_half.reshape(aux_count, row_count, occ_count).transpose(1, 0, 2)
    half = half.reshape(row_count, aux_count * occ_count).astype(jnp.bfloat16)
    aux_groups = lax.axis_size("aux")
    scale = 1.0 / math.sqrt(AUX_DEV * aux_groups * NOCC)
    every = lax.all_gather(half, "aux", axis=1, tiled=True)
    weighted_all = (every.astype(jnp.float32) * jnp.tile(weights, aux_count * aux_groups)).astype(
        jnp.bfloat16
    )
    spread = lax.axis_size("bas") // aux_groups
    first = lax.axis_index("aux") * spread
    received = [spread_2(every, "bas", first + offset) for offset in range(spread)]
    owned = jnp.concatenate(received, axis=0)
    per_group = aux_count * occ_count
    left = owned.reshape(owned.shape[0], aux_groups, per_group)
    right = weighted_all.reshape(row_count, aux_groups, per_group)
    terms = jnp.einsum("ngk,mgk->gnm", left, right, preferred_element_type=jnp.float32)
    rounded = lax.optimization_barrier(terms.astype(jnp.bfloat16))
    total = jnp.sum(rounded.astype(jnp.float32), axis=0)
    return (total * scale).astype(jnp.bfloat16)


def solution(mesh):
    in_specs = (P("aux", "bas", None), P("aux", "bas", None), P("bas", None), P())
    out_specs = P("aux", "bas")
    return jax.shard_map(shards, mesh=mesh, in_specs=in_specs, out_specs=out_specs, check_vma=False)
```

profile of v0, /device:TPU:0, one launch (start us, length us, event | category | flops | bytes accessed | tf_op | source)
XLA Modules:
  0.0 303.1 jit_solution(3715893133542091083)
XLA Ops:
  6.5 0.0 all-gather.3.cloned.1.call-start
  6.5 0.7 all-gather.3.cloned.1.call-update
  7.3 0.0 all-gather.5.cloned.1.call-start
  7.3 0.7 convert_bitcast_fusion
  8.0 49.4 %all-gather.3.cloned.1.call-done = bf16[8192,384]{1,0:T(8,128)(2,1)} async-done(((bf16[1024,384]{1,0:T(8,128)(2,1)}), bf16[8192,384]{1,0:T(8,128)(2,1)}) %all-gather.3.cloned.1.call-update) | async-done | bytes 6291472 | tf_op jit(solution)/shard_map/all_gather | solution.py:29
  57.4 6.5 %mul.33 = bf16[8,128,64,128]{3,2,1,0:T(8,128)(2,1)} broadcast(bf16[8,64]{1,0:T(8,128)(2,1)S(1)} %convert_bitcast_fusion), dimensions={0,2} | broadcast | bytes 16778240 | tf_op jit(solution)/shard_map/mul | solution.py:25
  63.8 26.9 %fusion.7 = bf16[1024,384]{1,0:T(8,128)(2,1)} fusion(bf16[8192,384]{1,0:T(8,128)(2,1)} %all-gather.3.cloned.1.call-done, bf16[128,8,64,128]{3,2,1,0:T(8,128)(2,1)} %bitcast.25, bf16[1,1024,8192]{2,1,0:T(8,128)(2,1)} %param.4), kind=kOutput, calls=%fused_computation.15 | convolution fusion | flops 6451232768 | bytes 40632320 | tf_op jit(solution)/shard_map/dot_general | solution.py:27
  90.7 0.0 all-gather.5.cloned.1.call-update
  90.7 0.2 all-reduce.3.cloned.1.call-start
  90.9 0.0 copy-start.2
  91.0 63.1 %all-gather.5.cloned.1.call-done = bf16[1024,1536]{1,0:T(8,128)(2,1)} async-done(((bf16[1024,384]{1,0:T(8,128)(2,1)}), bf16[1024,1536]{1,0:T(8,128)(2,1)}) %all-gather.5.cloned.1.call-update) | async-done | bytes 3145744 | tf_op jit(solution)/shard_map/all_gather | solution.py:36
  154.1 0.0 copy-start
  154.1 5.2 %broadcast_select_fusion.1 = (bf16[1024,1536]{1,0:T(8,128)(2,1)}, bf16[1024,1536]{1,0:T(8,128)(2,1)}) fusion(bf16[1024,1536]{1,0:T(8,128)(2,1)} %all-gather.5.cloned.1.call-done, pred[]{:T(512)S(6)} %eq.6, pred[]{:T(512)S(6)} %eq.7), kind=kLoop, calls=%fused_computation.14 | loop fusion | flops 3145728 | bytes 9437186 | tf_op jit(solution)/shard_map/jit(_where)/select_n | solution.py:13
  159.3 0.0 all-reduce.3.cloned.1.call-update
  159.3 0.0 copy-done.2
  159.3 0.0 copy-done
  159.3 2.3 multiply_convert_fusion.1
  161.6 100.4 %all-reduce.3.cloned.1.call-done = (bf16[1024,1536]{1,0:T(8,128)(2,1)}, bf16[1024,1536]{1,0:T(8,128)(2,1)}) async-done(((bf16[1024,1536]{1,0:T(8,128)(2,1)}, bf16[1024,1536]{1,0:T(8,128)(2,1)}), (bf16[1024,1536]{1,0:T(8,128)(2,1)}, bf16[1024,1536]{1,0:T(8,128)(2,1)})) %all-reduce.3.cloned.1.call-update) | async-done | bytes 6291472 | tf_op jit(solution)/shard_map/psum | solution.py:14
  262.0 0.0 copy-start.1
  262.0 6.1 %pad_maximum_fusion = bf16[2048,1536]{1,0:T(8,128)(2,1)} fusion(bf16[1024,1536]{1,0:T(8,128)(2,1)} %get-tuple-element.5, bf16[1024,1536]{1,0:T(8,128)(2,1)} %get-tuple-element.6), kind=kLoop, calls=%fused_computation.9 | loop fusion | flops 12582912 | bytes 12582912 | tf_op jit(solution)/shard_map/concatenate | solution.py:43
  268.0 0.0 copy-done.1
  268.0 15.3 %convolution_convert_fusion = bf16[4,2048,1024]{2,1,0:T(8,128)(2,1)} fusion(bf16[256,4,8,384]{3,2,1,0:T(8,128)(2,1)} %bitcast.26, bf16[128,4,8,384]{3,2,1,0:T(8,128)(2,1)S(1)} %bitcast.27), kind=kOutput, calls=%fused_computation.5 | convolution fusion | flops 6450839552 | bytes 26214400 | tf_op jit(solution)/shard_map/ngk,mgk->gnm/dot_general | solution.py:47
  283.3 9.8 %convert_reduce_fusion = f32[2048,1024]{1,0:T(8,128)S(1)} fusion(bf16[4,2048,1024]{2,1,0:T(8,128)(2,1)} %convolution_convert_fusion), kind=kLoop, calls=%fused_computation | loop fusion | flops 14680064 | bytes 25165824 | tf_op jit(solution)/shard_map/reduce_sum | solution.py:49
  293.2 3.4 %multiply_convert_fusion = bf16[2048,1024]{1,0:T(8,128)(2,1)} fusion(f32[2048,1024]{1,0:T(8,128)S(1)} %convert_reduce_fusion), kind=kLoop, calls=%fused_computation.6 | loop fusion | flops 4194304 | bytes 12582912 | tf_op jit(solution)/shard_map/convert_element_type | solution.py:50
  (2 shorter events, 0.0 us)
Async XLA Ops:
  6.5 50.8 %all-gather.3.cloned.1.call-start = ((), (), s32[]{:S(2)}) async-start(), calls=%async_computation | async-start | bytes 7077888 | tf_op jit(solution)/shard_map/all_gather | solution.py:29
  7.3 146.8 %all-gather.5.cloned.1.call-start = ((), (), s32[]{:S(2)}) async-start(), calls=%async_computation.1 | async-start | bytes 3932160 | tf_op jit(solution)/shard_map/all_gather | solution.py:36
  90.7 171.3 %all-reduce.3.cloned.1.call-start = ((), (), s32[]{:S(2)}) async-start(), calls=%async_computation.2 | async-start | bytes 12582912 | tf_op jit(solution)/shard_map/psum | solution.py:14
  90.9 68.3 %copy-start.2 = (f32[384]{0:T(512)S(1)}, f32[384]{0:T(512)}, u32[]{:S(2)}) copy-start(f32[384]{0:T(512)} %param.7) | copy-start | bytes 4612
  154.1 5.2 %copy-start = (bf16[1024,1536]{1,0:T(8,128)(2,1)S(1)}, bf16[1024,1536]{1,0:T(8,128)(2,1)}, u32[]{:S(2)}) copy-start(bf16[1024,1536]{1,0:T(8,128)(2,1)} %all-gather.5.cloned.1.call-done) | copy-start | bytes 9437188
  262.0 6.1 %copy-start.1 = (bf16[1024,1536]{1,0:T(8,128)(2,1)S(1)}, bf16[1024,1536]{1,0:T(8,128)(2,1)}, u32[]{:S(2)}) copy-start(bf16[1024,1536]{1,0:T(8,128)(2,1)} %multiply_convert_fusion.1) | copy-start | bytes 9437188
Sparse Core Ops, SparseCore 0:
  9.2 48.1 all-gather.2
  90.8 63.2 all-gather.4
  159.4 102.5 all-reduce.2
where the time goes:
time: 303 us
  waiting for transfers between devices  214 us (71%)
  matrix products  42.1 us (14%)
  other arithmetic  27.4 us (9%)
  between operations  13.2 us (4%)
  local copies, waits for them, and re-layouts  6.49 us (2%)
    psum x1, waiting for transfers between devices, spread_2(): return lax.psum(block, axis)  100 us
    all_gather x1, waiting for transfers between devices, shards(): every = lax.all_gather(half, 'aux', axis=1, tiled=True)  63.1 us
    all_gather x1, waiting for transfers between devices, shards(): lax.all_gather(coefficients, 'bas', axis=0, tiled=True)  49.4 us
    dot_general x1, matrix products, shards(): jnp.dot(flat, lax.all_gather(coefficients, 'bas', axis=0, tiled=True), pr...  26.9 us
    dot_general x1, matrix products, shards(): jnp.einsum('ngk,mgk->gnm', left, right, preferred_element_type=jnp.float32)  15.3 us
    reduce_sum x1, other arithmetic, shards(): total = jnp.sum(rounded.astype(jnp.float32), axis=0)  9.83 us
    mul x1, local copies, waits for them, and re-layouts, shards(): integrals.reshape(aux_count, row_blocks, BLOCK, col_blocks, BLOCK) * masks  6.46 us
  transfers between devices with their start and end apart: 3, of which 3 were waited for; matrix products, arithmetic and copies ran while one was open for 1% of the time, Pallas kernels for 0%

commit v1 on v0

--- a/solution.py
+++ b/solution.py
@@ -11,7 +11,7 @@
 
 def spread_2(block, axis, owner):
     block = jnp.where(lax.axis_index(axis) == owner, block, jnp.zeros_like(block))
-    return lax.psum(block, axis)
+    return jnp.sum(lax.all_gather(block, axis), axis=0)
 
 
 def shards(integrals, screen, coefficients, weights):

time: 303 us -> 476 us (1.57)
  waiting for transfers between devices: 214 us -> 347 us
  other arithmetic: 27.4 us -> 56.6 us
  local copies, waits for them, and re-layouts: 6.49 us -> 15.3 us
    all_gather x0 -> x2, waiting for transfers between devices: none -> 233 us  [spread_2(): return jnp.sum(lax.all_gather(block, axis), axis=0)]
    psum x1 -> x0, waiting for transfers between devices: 100 us -> none  [spread_2(): return lax.psum(block, axis)]
    reduce_sum x0 -> x2, other arithmetic: none -> 30.4 us  [spread_2(): return jnp.sum(lax.all_gather(block, axis), axis=0)]
    concatenate x0 -> x1, local copies, waits for them, and re-layouts: none -> 8.76 us  [shards(): owned = jnp.concatenate(received, axis=0)]
  transfers between devices with their start and end apart: 3 -> 4, of which waited for: 3 -> 4; matrix products, arithmetic and copies ran while one was open for 1% -> 4% of each run, Pallas kernels for 0% -> 0%
where the time goes in v1:
time: 476 us; the launch traced here: 475 us
  waiting for transfers between devices  347 us (73%)
  other arithmetic  56.6 us (12%)
  matrix products  43.1 us (9%)
  local copies, waits for them, and re-layouts  15.3 us (3%)
  between operations  13.2 us (3%)
    all_gather x2, waiting for transfers between devices, spread_2(): return jnp.sum(lax.all_gather(block, axis), axis=0)  233 us
    all_gather x1, waiting for transfers between devices, shards(): every = lax.all_gather(half, 'aux', axis=1, tiled=True)  63.3 us
    all_gather x1, waiting for transfers between devices, shards(): lax.all_gather(coefficients, 'bas', axis=0, tiled=True)  49.4 us
    reduce_sum x2, other arithmetic, spread_2(): return jnp.sum(lax.all_gather(block, axis), axis=0)  30.4 us
    dot_general x1, matrix products, shards(): jnp.dot(flat, lax.all_gather(coefficients, 'bas', axis=0, tiled=True), pr...  26.8 us
    dot_general x1, matrix products, shards(): jnp.einsum('ngk,mgk->gnm', left, right, preferred_element_type=jnp.float32)  16.2 us
    reduce_sum x1, other arithmetic, shards(): total = jnp.sum(rounded.astype(jnp.float32), axis=0)  9.83 us
  transfers between devices with their start and end apart: 4, of which 4 were waited for; matrix products, arithmetic and copies ran while one was open for 4% of the time, Pallas kernels for 0%

profile of v1, /device:TPU:0, one launch (start us, length us, event | category | flops | bytes accessed | tf_op | source)
XLA Modules:
  0.0 475.3 jit_solution(13883535933825530539)
XLA Ops:
  6.5 0.0 all-gather.7.cloned.1.call-start
  6.5 0.7 all-gather.7.cloned.1.call-update
  7.3 0.0 all-gather.9.cloned.1.call-start
  7.3 0.7 convert_bitcast_fusion
  8.0 49.4 %all-gather.7.cloned.1.call-done = bf16[8192,384]{1,0:T(8,128)(2,1)} async-done(((bf16[1024,384]{1,0:T(8,128)(2,1)}), bf16[8192,384]{1,0:T(8,128)(2,1)}) %all-gather.7.cloned.1.call-update) | async-done | bytes 6291472 | tf_op jit(solution)/shard_map/all_gather | solution.py:29
  57.4 6.5 %mul.33 = bf16[8,128,64,128]{3,2,1,0:T(8,128)(2,1)} broadcast(bf16[8,64]{1,0:T(8,128)(2,1)S(1)} %convert_bitcast_fusion), dimensions={0,2} | broadcast | bytes 16778240 | tf_op jit(solution)/shard_map/mul | solution.py:25
  63.8 26.8 %fusion.5 = bf16[1024,384]{1,0:T(8,128)(2,1)} fusion(bf16[8192,384]{1,0:T(8,128)(2,1)} %all-gather.7.cloned.1.call-done, bf16[128,8,64,128]{3,2,1,0:T(8,128)(2,1)} %bitcast.27, bf16[1,1024,8192]{2,1,0:T(8,128)(2,1)} %param.4), kind=kOutput, calls=%fused_computation.13 | convolution fusion | flops 6451232768 | bytes 40632320 | tf_op jit(solution)/shard_map/dot_general | solution.py:27
  90.7 0.0 all-gather.9.cloned.1.call-update
  90.7 0.0 all-gather.11.cloned.1.call-start
  90.8 0.0 copy-start.2
  90.8 63.3 %all-gather.9.cloned.1.call-done = bf16[1024,1536]{1,0:T(8,128)(2,1)} async-done(((bf16[1024,384]{1,0:T(8,128)(2,1)}), bf16[1024,1536]{1,0:T(8,128)(2,1)}) %all-gather.9.cloned.1.call-update) | async-done | bytes 3145744 | tf_op jit(solution)/shard_map/all_gather | solution.py:36
  154.1 0.0 copy-start
  154.1 5.1 %broadcast_select_fusion.1 = (bf16[1024,1536]{1,0:T(8,128)(2,1)}, bf16[1024,1536]{1,0:T(8,128)(2,1)}) fusion(bf16[1024,1536]{1,0:T(8,128)(2,1)} %all-gather.9.cloned.1.call-done, pred[]{:T(512)S(6)} %eq.6, pred[]{:T(512)S(6)} %eq.7), kind=kLoop, calls=%fused_computation.12 | loop fusion | flops 3145728 | bytes 9437186 | tf_op jit(solution)/shard_map/jit(_where)/select_n | solution.py:13
  159.2 0.0 all-gather.11.cloned.1.call-update
  159.2 0.2 all-gather.13.cloned.1.call-start
  159.4 0.3 all-gather.13.cloned.1.call-update
  159.8 0.0 copy-done.2
  159.8 0.0 copy-done
  159.8 2.2 multiply_convert_fusion.1
  162.1 121.1 %all-gather.11.cloned.1.call-done = bf16[8192,1536]{1,0:T(8,128)(2,1)} async-done(((bf16[1024,1536]{1,0:T(8,128)(2,1)}), bf16[8192,1536]{1,0:T(8,128)(2,1)}) %all-gather.11.cloned.1.call-update) | async-done | bytes 25165840 | tf_op jit(solution)/shard_map/all_gather | solution.py:14
  283.2 14.9 %reduce_sum.33 = bf16[1024,1536]{1,0:T(8,128)(2,1)S(1)} reduce(bf16[8,1024,1536]{2,1,0:T(8,128)(2,1)} %bitcast.25, bf16[]{:T(256)} %constant.17.clone.1), dimensions={0}, to_apply=%region_0.1 | reduce | flops 11010048 | bytes 28311554 | tf_op jit(solution)/shard_map/reduce_sum | solution.py:14
  298.1 112.0 %all-gather.13.cloned.1.call-done = bf16[8192,1536]{1,0:T(8,128)(2,1)} async-done(((bf16[1024,1536]{1,0:T(8,128)(2,1)}), bf16[8192,1536]{1,0:T(8,128)(2,1)}) %all-gather.13.cloned.1.call-update) | async-done | bytes 25165840 | tf_op jit(solution)/shard_map/all_gather | solution.py:14
  410.1 15.5 %reduce_sum.34 = bf16[1024,1536]{1,0:T(8,128)(2,1)} reduce(bf16[8,1024,1536]{2,1,0:T(8,128)(2,1)} %bitcast.26, bf16[]{:T(256)} %constant.17.clone.1), dimensions={0}, to_apply=%region_1.2 | reduce | flops 11010048 | bytes 28311554 | tf_op jit(solution)/shard_map/reduce_sum | solution.py:14
  425.6 5.0 %pad_maximum_fusion = bf16[2048,1536]{1,0:T(8,128)(2,1)} fusion(bf16[1024,1536]{1,0:T(8,128)(2,1)} %reduce_sum.34, bf16[1024,1536]{1,0:T(8,128)(2,1)S(1)} %reduce_sum.33), kind=kLoop, calls=%fused_computation.7 | loop fusion | flops 12582912 | bytes 12582912 | tf_op jit(solution)/shard_map/concatenate | solution.py:43
  430.5 0.0 copy-start.1
  430.5 8.8 %copy.8 = bf16[2048,1536]{0,1:T(8,128)(2,1)} copy(bf16[2048,1536]{1,0:T(8,128)(2,1)} %pad_maximum_fusion) | data formatting | bytes 12582912 | tf_op jit(solution)/shard_map/concatenate | solution.py:43
  439.3 0.0 copy-done.1
  439.3 16.2 %convolution_convert_fusion = bf16[4,2048,1024]{2,1,0:T(8,128)(2,1)} fusion(bf16[2048,4,384]{0,2,1:T(8,128)(2,1)} %bitcast.28, bf16[128,4,8,384]{3,2,1,0:T(8,128)(2,1)S(1)} %bitcast.29), kind=kOutput, calls=%fused_computation.5 | convolution fusion | flops 6450839552 | bytes 26214400 | tf_op jit(solution)/shard_map/ngk,mgk->gnm/dot_general | solution.py:47
  455.5 9.8 %convert_reduce_fusion = f32[2048,1024]{1,0:T(8,128)S(1)} fusion(bf16[4,2048,1024]{2,1,0:T(8,128)(2,1)} %convolution_convert_fusion), kind=kLoop, calls=%fused_computation | loop fusion | flops 14680064 | bytes 25165824 | tf_op jit(solution)/shard_map/reduce_sum | solution.py:49
  465.4 3.4 multiply_convert_fusion
  (2 shorter events, 0.0 us)
Async XLA Ops:
  6.5 50.8 %all-gather.7.cloned.1.call-start = ((), (), s32[]{:S(2)}) async-start(), calls=%async_computation | async-start | bytes 7077888 | tf_op jit(solution)/shard_map/all_gather | solution.py:29
  7.3 146.8 %all-gather.9.cloned.1.call-start = ((), (), s32[]{:S(2)}) async-start(), calls=%async_computation.1 | async-start | bytes 3932160 | tf_op jit(solution)/shard_map/all_gather | solution.py:36
  90.7 192.5 %all-gather.11.cloned.1.call-start = ((), (), s32[]{:S(2)}) async-start(), calls=%async_computation.2 | async-start | bytes 28311552 | tf_op jit(solution)/shard_map/all_gather | solution.py:14
  90.8 69.0 %copy-start.2 = (f32[384]{0:T(512)S(1)}, f32[384]{0:T(512)}, u32[]{:S(2)}) copy-start(f32[384]{0:T(512)} %param.7) | copy-start | bytes 4612
  154.1 5.7 %copy-start = (bf16[1024,1536]{1,0:T(8,128)(2,1)S(1)}, bf16[1024,1536]{1,0:T(8,128)(2,1)}, u32[]{:S(2)}) copy-start(bf16[1024,1536]{1,0:T(8,128)(2,1)} %all-gather.9.cloned.1.call-done) | copy-start | bytes 9437188
  159.2 250.9 %all-gather.13.cloned.1.call-start = ((), (), s32[]{:S(2)}) async-start(), calls=%async_computation.3 | async-start | bytes 28311552 | tf_op jit(solution)/shard_map/all_gather | solution.py:14
  430.5 8.8 %copy-start.1 = (bf16[1024,1536]{1,0:T(8,128)(2,1)S(1)}, bf16[1024,1536]{1,0:T(8,128)(2,1)}, u32[]{:S(2)}) copy-start(bf16[1024,1536]{1,0:T(8,128)(2,1)} %multiply_convert_fusion.1) | copy-start | bytes 9437188
Sparse Core Ops, SparseCore 0:
  9.2 48.1 all-gather.6
  90.8 63.2 all-gather.8
  159.3 123.7 all-gather.10
  284.9 125.1 all-gather.12
